TPU v7x, 32 devices: a whole 2x2x4 slice. The times are simulated.
32 devices in a mesh: row: 8 (over z, y), col: 4 (over x, core).
Axes of the slice: x: 2, y: 2, z: 4, core: 2. Of those that a mesh axis runs over, the one named last changes fastest.
Arguments:
- upper: bfloat16 [4096, 8, 4, 128], P('row', None, 'col'), as said below
- signs: int32 [4096, 512], P(('row', 'col')), may hold values from 0 to 1
- weights: float32 [4096], P(('row', 'col')), may hold values from 0.5 to 2
- components: float32 [2], replicated, may hold values from 0.3 to 3
Outputs:
- applied: float32 [4096, 512], P(('row', 'col'))
Inputs may be any that keep to these rules, and one draw needn't show every extreme that they name: upper's first dimension and its flattened column index count the same samples in the same order.
All inputs are finite; a program needn't handle non-finite values.
Results may differ from a plain program's by a relative error of at most 0.0055.
Values may be sent and summed in bfloat16 or wider, within the bound.
No kernel may reach another device: no remote copies, remote signals or barrier semaphores. Data moves between devices by JAX's collectives and lax.ppermute only.
A program may use at most 128 MiB of HBM per device.

v0:
```python
import jax
import jax.numpy as jnp
from jax import lax
from jax.sharding import PartitionSpec as P


def body(upper, signs, weights, components):
    rows, ntiles, single, fine = upper.shape
    row_index = lax.axis_index("row")
    col_index = lax.axis_index("col")
    flat = upper.reshape(rows, ntiles * fine)
    probes = ((2 * signs - 1).astype(jnp.float32) * weights[:, None]).astype(jnp.bfloat16)
    q_rows = lax.all_gather(probes, "col", axis=0, tiled=True)
    zero = jnp.zeros((), jnp.bfloat16)
    rowpos = lax.broadcasted_iota(jnp.int32, (rows, ntiles, fine), 0)
    tilepos = lax.broadcasted_iota(jnp.int32, (rows, ntiles, fine), 1)
    colpos = col_index * fine + lax.broadcasted_iota(jnp.int32, (rows, ntiles, fine), 2)
    beyond = tilepos > row_index
    onside = tilepos == row_index
    keep_up = (beyond | onside & (colpos >= rowpos)).reshape(rows, ntiles * fine)
    keep_strict = (beyond | onside & (colpos > rowpos)).reshape(rows, ntiles * fine)
    masked_a = jnp.where(keep_up, flat, zero)
    masked_b = jnp.where(keep_strict, flat, zero)
    columns = masked_a
    direct = jnp.dot(
        columns,
        lax.all_gather(probes, "row", axis=0, tiled=True),
        preferred_element_type=jnp.float32,
    )
    columns = masked_b
    mirrored = lax.psum_scatter(
        lax.dot_general(
            columns, q_rows, (((0,), (0,)), ((), ())), preferred_element_type=jnp.float32
        ).astype(jnp.bfloat16),
        "row",
        scatter_dimension=0,
        tiled=True,
    ).astype(jnp.float32)
    summed = lax.psum_scatter(direct, "col", scatter_dimension=0, tiled=True)
    return components[0] * (summed + mirrored) + components[1] * probes.astype(jnp.float32)


def solution(mesh):
    return jax.shard_map(
        body,
        mesh=mesh,
        in_specs=(P("row", None, "col", None), P(("row", "col"), None), P(("row", "col")), P()),
        out_specs=P(("row", "col"), None),
        check_vma=False,
    )
```

profile of v0, /device:TPU:0, one launch (start us, length us, event | category | flops | bytes accessed | tf_op | source)
XLA Modules:
  0.0 154.1 jit_solution(2603484826157275666)
XLA Ops:
  6.5 0.0 copy-start.3
  6.5 0.0 all-gather.2.cloned.1.call-start
  6.5 1.8 %multiply_convert_fusion = bf16[128,512]{1,0:T(8,128)(2,1)} fusion(s32[128,512]{1,0:T(8,128)} %param.5, f32[128]{0:T(128)} %param.6), kind=kLoop, calls=%fused_computation.23 | loop fusion | flops 327680 | bytes 393728 | tf_op jit(solution)/shard_map/convert_element_type | solution.py:12
  8.3 0.0 all-gather.2.cloned.1.call-update
  8.3 0.0 reduce-scatter.5.cloned.1.call-start
  8.4 8.8 %all_gather.7 = bf16[512,512]{1,0:T(8,128)(2,1)S(1)} all-gather(bf16[128,512]{1,0:T(8,128)(2,1)} %multiply_convert_fusion), channel_id=1, replica_groups=mesh['row'=8,'col'=4] {'col'}, dimensions={0}, use_global_device_ids=true | all-gather | bytes 655360 | tf_op jit(solution)/shard_map/all_gather | solution.py:13
  17.3 0.1 broadcast_bitcast_fusion.1
  17.3 0.1 broadcast_bitcast_fusion.2
  17.4 0.0 copy-done.3
  17.4 1.8 %convolution_convert_fusion = bf16[1024,512]{1,0:T(8,128)(2,1)} fusion(bf16[512,512]{1,0:T(8,128)(2,1)S(1)} %all_gather.7, s32[1024]{0:T(1024)S(1)} %broadcast_bitcast_fusion, pred[1024]{0:T(1024)(128)(4,1)S(1)} %broadcast_bitcast_fusion.1, pred[1024]{0:T(1024)(128)(4,1)S(1)} %broadcast_bitcast_fusion.2, bf16[64,8,8,128]{3,2,1,0:T(8,128)(2,1)S(1)} %bitcast.22), kind=kOutput, calls=%fused_computation.8 | convolution fusion | flops 539492352 | bytes 2627584 | tf_op jit(solution)/shard_map/dot_general | solution.py:32
  19.2 0.0 reduce-scatter.5.cloned.1.call-update
  19.2 0.0 reduce-scatter.3.cloned.1.call-start
  19.3 33.1 %all-gather.2.cloned.1.call-done = bf16[1024,512]{1,0:T(8,128)(2,1)} async-done(((bf16[128,512]{1,0:T(8,128)(2,1)}), bf16[1024,512]{1,0:T(8,128)(2,1)}) %all-gather.2.cloned.1.call-update) | async-done | bytes 1048592 | tf_op jit(solution)/shard_map/all_gather | solution.py:27
  52.4 3.0 %fusion.7 = f32[512,512]{1,0:T(8,128)} fusion(bf16[1024,512]{1,0:T(8,128)(2,1)} %all-gather.2.cloned.1.call-done, s32[1024]{0:T(1024)S(1)} %broadcast_bitcast_fusion, pred[1024]{0:T(1024)(128)(4,1)S(1)} %broadcast_bitcast_fusion.1, pred[1024]{0:T(1024)(128)(4,1)S(1)} %broadcast_bitcast_fusion.2, bf16[64,8,8,128]{3,2,1,0:T(8,128)(2,1)S(1)} %bitcast.23), kind=kOutput, calls=%fused_computation.9 | convolution fusion | flops 538968064 | bytes 3151872 | tf_op jit(solution)/shard_map/dot_general | solution.py:25
  55.3 0.0 copy-start.2
  55.3 0.0 copy-start
  55.3 0.0 reduce-scatter.3.cloned.1.call-update
  55.4 0.6 copy-done.2
  56.0 0.6 fusion.23
  56.6 61.3 %reduce-scatter.5.cloned.1.call-done = bf16[128,512]{1,0:T(8,128)(2,1)} async-done(((bf16[1024,512]{1,0:T(8,128)(2,1)}), bf16[128,512]{1,0:T(8,128)(2,1)}) %reduce-scatter.5.cloned.1.call-update) | async-done | bytes 131088 | tf_op jit(solution)/shard_map/reduce_scatter | solution.py:31
  117.9 26.6 %reduce-scatter.3.cloned.1.call-done = f32[128,512]{1,0:T(8,128)} async-done(((f32[512,512]{1,0:T(8,128)}), f32[128,512]{1,0:T(8,128)}) %reduce-scatter.3.cloned.1.call-update) | async-done | bytes 262160 | tf_op jit(solution)/shard_map/reduce_scatter | solution.py:39
  144.5 0.0 copy-done
  144.5 0.0 copy-done.1
  144.5 3.1 %multiply_add_fusion = f32[128,512]{1,0:T(8,128)} fusion(f32[128,512]{1,0:T(8,128)} %reduce-scatter.3.cloned.1.call-done, bf16[128,512]{1,0:T(8,128)(2,1)} %reduce-scatter.5.cloned.1.call-done, f32[]{:T(128)} %bitcast.4, f32[]{:T(128)} %bitcast, f32[128]{0:T(128)S(1)} %copy-done.1, s32[128,512]{1,0:T(8,128)S(1)} %copy-done), kind=kLoop, calls=%fused_computation.22 | loop fusion | flops 720896 | bytes 918024 | tf_op jit(solution)/shard_map/add | solution.py:40
  (4 shorter events, 0.0 us)
Async XLA Ops:
  6.5 10.9 %copy-start.3 = (bf16[512,8,1,128]{3,1,2,0:T(8,128)(2,1)S(1)}, bf16[512,8,1,128]{3,1,2,0:T(8,128)(2,1)}, u32[]{:S(2)}) copy-start(bf16[512,8,1,128]{3,1,2,0:T(8,128)(2,1)} %param.4) | copy-start | bytes 3145732
  6.5 45.8 %all-gather.2.cloned.1.call-start = ((), (), s32[]{:S(2)}) async-start(), calls=%async_computation.2 | async-start | bytes 1179648 | tf_op jit(solution)/shard_map/all_gather | solution.py:27
  8.3 109.5 %reduce-scatter.5.cloned.1.call-start = ((), (), s32[]{:S(2)}) async-start(), calls=%async_computation.4 | async-start | bytes 1179648 | tf_op jit(solution)/shard_map/reduce_scatter | solution.py:31
  19.2 125.3 %reduce-scatter.3.cloned.1.call-start = ((), (), s32[]{:S(2)}) async-start(), calls=%async_computation.3 | async-start | bytes 1310720 | tf_op jit(solution)/shard_map/reduce_scatter | solution.py:39
  55.3 0.7 copy-start.2
  55.3 89.2 %copy-start = (s32[128,512]{1,0:T(8,128)S(1)}, s32[128,512]{1,0:T(8,128)}, u32[]{:S(2)}) copy-start(s32[128,512]{1,0:T(8,128)} %param.5) | copy-start | bytes 786436
  55.3 89.2 %copy-start.1 = (f32[128]{0:T(128)S(1)}, f32[128]{0:T(128)}, u32[]{:S(2)}) copy-start(f32[128]{0:T(128)} %param.6) | copy-start | bytes 1540
Sparse Core Ops, SparseCore 0:
  9.5 42.8 all-gather.1
  55.8 62.0 reduce-scatter.4
  120.6 23.8 reduce-scatter.2
where the time goes:
time: 154 us
  waiting for transfers between devices  121 us (79%)
  between operations  13.1 us (9%)
  blocking collectives  8.83 us (6%)
  other arithmetic  4.85 us (3%)
  matrix products  4.75 us (3%)
    reduce_scatter x1, waiting for transfers between devices, body(): lax.psum_scatter(lax.dot_general(columns, q_rows, (((0,), (0,)), ((), ())...  61.3 us
    all_gather x1, waiting for transfers between devices, body(): lax.all_gather(probes, 'row', axis=0, tiled=True)  33.1 us
    reduce_scatter x1, waiting for transfers between devices, body(): summed = lax.psum_scatter(direct, 'col', scatter_dimension=0, tiled=True)  26.6 us
    all_gather x1, blocking collectives, body(): q_rows = lax.all_gather(probes, 'col', axis=0, tiled=True)  8.83 us
  transfers between devices with their start and end apart: 3, of which 3 were waited for; matrix products, arithmetic and copies ran while one was open for 4% of the time, Pallas kernels for 0%

commit v1 on v0

--- a/solution.py
+++ b/solution.py
@@ -1,7 +1,23 @@
+import functools
 import jax
 import jax.numpy as jnp
 from jax import lax
 from jax.sharding import PartitionSpec as P
+
+
+def move_column_up(xx, in_dim):
+    q_next, p_next, back = (lax.axis_size("row"), lax.axis_index("row"), xx.shape[in_dim])
+    k_now, lower = (xx, 1)
+    while lower < q_next:
+        k_now = jnp.concatenate(
+            [k_now, lax.ppermute(k_now, "row", [(c, (c - lower) % q_next) for c in range(q_next)])],
+            axis=in_dim,
+        )
+        lower = 2 * lower
+    return jnp.roll(k_now, p_next * back, axis=in_dim)
+
+
+expand_sheets = functools.partial(move_column_up, in_dim=0)
 
 
 def body(upper, signs, weights, components):
@@ -22,11 +38,7 @@
     masked_a = jnp.where(keep_up, flat, zero)
     masked_b = jnp.where(keep_strict, flat, zero)
     columns = masked_a
-    direct = jnp.dot(
-        columns,
-        lax.all_gather(probes, "row", axis=0, tiled=True),
-        preferred_element_type=jnp.float32,
-    )
+    direct = jnp.dot(columns, expand_sheets(probes), preferred_element_type=jnp.float32)
     columns = masked_b
     mirrored = lax.psum_scatter(
         lax.dot_general(

time: 154 us -> 137 us (0.89)
  waiting for transfers between devices: 121 us -> 91.7 us
  starting transfers between devices: 0.09 us -> 6.3 us
  local copies, waits for them, and re-layouts: 1.39 us -> 5.94 us
    ppermute x0 -> x3, waiting for transfers between devices: none -> 40.4 us  [move_column_up(): lax.ppermute(k_now, 'row', [(c, (c - lower) % q_next) for c in range(q_ne...]
    reduce_scatter x1, waiting for transfers between devices: 61.3 us -> 24.6 us  [body(): lax.psum_scatter(lax.dot_general(columns, q_rows, (((0,), (0,)), ((), ())...]
    all_gather x1 -> x0, waiting for transfers between devices: 33.1 us -> none  [body(): lax.all_gather(probes, 'row', axis=0, tiled=True)]
    ppermute x0 -> x3, starting transfers between devices: none -> 6.26 us  [move_column_up(): lax.ppermute(k_now, 'row', [(c, (c - lower) % q_next) for c in range(q_ne...]
    unnamed x8 -> x10, local copies, waits for them, and re-layouts: 0.64 us -> 4.29 us
    convert_element_type x1 -> x0, other arithmetic: 1.78 us -> none  [body(): ((2 * signs - 1).astype(jnp.float32) * weights[:, None]).astype(jnp.bfloa...]
    unnamed x0 -> x1, other arithmetic: none -> 1.71 us
  transfers between devices with their start and end apart: 3 -> 5, of which waited for: 3 -> 5; matrix products, arithmetic and copies ran while one was open for 4% -> 6% of each run, Pallas kernels for 0% -> 0%
where the time goes in v1:
time: 137 us
  waiting for transfers between devices  91.7 us (67%)
  between operations  13.5 us (10%)
  blocking collectives  8.6 us (6%)
  starting transfers between devices  6.3 us (5%)
  matrix products  5.98 us (4%)
  local copies, waits for them, and re-layouts  5.94 us (4%)
  other arithmetic  4.82 us (4%)
    ppermute x3, waiting for transfers between devices, move_column_up(): lax.ppermute(k_now, 'row', [(c, (c - lower) % q_next) for c in range(q_ne...  40.4 us
    reduce_scatter x1, waiting for transfers between devices, body(): summed = lax.psum_scatter(direct, 'col', scatter_dimension=0, tiled=True)  26.6 us
    reduce_scatter x1, waiting for transfers between devices, body(): lax.psum_scatter(lax.dot_general(columns, q_rows, (((0,), (0,)), ((), ())...  24.6 us
    all_gather x1, blocking collectives, body(): q_rows = lax.all_gather(probes, 'col', axis=0, tiled=True)  8.6 us
    ppermute x3, starting transfers between devices, move_column_up(): lax.ppermute(k_now, 'row', [(c, (c - lower) % q_next) for c in range(q_ne...  6.26 us
    unnamed x10, local copies, waits for them, and re-layouts  4.29 us
    add x1, other arithmetic, body(): components[0] * (summed + mirrored)  3.05 us
    dot_general x1, matrix products, body(): lax.dot_general(columns, q_rows, (((0,), (0,)), ((), ())), preferred_elem...  3.03 us
  transfers between devices with their start and end apart: 5, of which 5 were waited for; matrix products, arithmetic and copies ran while one was open for 6% of the time, Pallas kernels for 0%

profile of v1, /device:TPU:0, one launch (start us, length us, event | category | flops | bytes accessed | tf_op | source)
XLA Modules:
  0.0 136.8 jit_solution(1946478852003145615)
XLA Ops:
  6.5 0.1 broadcast_bitcast_fusion.1
  6.6 0.1 broadcast_bitcast_fusion.2
  6.7 1.7 %constant_dynamic-update-slice_fusion.7 = (bf16[2048,512]{1,0:T(8,128)(2,1)}, bf16[128,512]{1,0:T(8,128)(2,1)S(1)}) fusion(f32[128]{0:T(128)} %param.6, s32[128,512]{1,0:T(8,128)} %param.5), kind=kLoop, calls=%fused_computation.34 | loop fusion | flops 327679 | bytes 524800
  8.4 8.6 %all_gather.3 = bf16[512,512]{1,0:T(8,128)(2,1)S(1)} all-gather(bf16[128,512]{1,0:T(8,128)(2,1)S(1)} %get-tuple-element.6), channel_id=1, replica_groups=mesh['row'=8,'col'=4] {'col'}, dimensions={0}, use_global_device_ids=true | all-gather | bytes 655360 | tf_op jit(solution)/shard_map/all_gather | solution.py:29
  17.0 3.0 %convolution_convert_fusion = bf16[1024,512]{1,0:T(8,128)(2,1)} fusion(bf16[512,512]{1,0:T(8,128)(2,1)S(1)} %all_gather.3, s32[1024]{0:T(1024)S(1)} %broadcast_bitcast_fusion, pred[1024]{0:T(1024)(128)(4,1)S(1)} %broadcast_bitcast_fusion.1, pred[1024]{0:T(1024)(128)(4,1)S(1)} %broadcast_bitcast_fusion.2, bf16[64,8,8,128]{3,2,1,0:T(8,128)(2,1)} %bitcast.21), kind=kOutput, calls=%fused_computation.8 | convolution fusion | flops 539492352 | bytes 2627584 | tf_op jit(solution)/shard_map/dot_general | solution.py:44
  20.1 0.0 reduce-scatter.3.cloned.1.call-start
  20.1 4.6 %collective-permute-start = (bf16[128,512]{1,0:T(8,128)(2,1)S(1)}, bf16[128,512]{1,0:T(8,128)(2,1)S(1)}, u32[]{:S(2)}, u32[]{:S(2)}) collective-permute-start(bf16[128,512]{1,0:T(8,128)(2,1)S(1)} %get-tuple-element.6), channel_id=1, source_target_pairs={{0,28},{4,0},{8,4},{12,8},{16,12},{20,16},{24,20},{28,24},{1,29},{... | collective-permute-start | bytes 393224 | tf_op jit(solution)/shard_map/ppermute | solution.py:13
  24.7 3.3 %collective-permute-done = bf16[128,512]{1,0:T(8,128)(2,1)S(1)} collective-permute-done((bf16[128,512]{1,0:T(8,128)(2,1)S(1)}, bf16[128,512]{1,0:T(8,128)(2,1)S(1)}, u32[]{:S(2)}, u32[]{:S(2)}) %collective-permute-start) | collective-permute-done | bytes 131104 | tf_op jit(solution)/shard_map/ppermute | solution.py:13
  28.0 1.6 %collective-permute-start.1 = (bf16[256,512]{1,0:T(8,128)(2,1)S(1)}, bf16[256,512]{1,0:T(8,128)(2,1)S(1)}, u32[]{:S(2)}, u32[]{:S(2)}) collective-permute-start(bf16[256,512]{1,0:T(8,128)(2,1)S(1)} %pad_maximum_fusion.1), channel_id=1, source_target_pairs={{0,24},{4,28},{8,0},{12,4},{16,8},{20,12},{24,16},{28,20},{1,25},{... | collective-permute-start | bytes 786440 | tf_op jit(solution)/shard_map/ppermute | solution.py:13
  29.6 9.8 %collective-permute-done.1 = bf16[256,512]{1,0:T(8,128)(2,1)S(1)} collective-permute-done((bf16[256,512]{1,0:T(8,128)(2,1)S(1)}, bf16[256,512]{1,0:T(8,128)(2,1)S(1)}, u32[]{:S(2)}, u32[]{:S(2)}) %collective-permute-start.1) | collective-permute-done | bytes 262176 | tf_op jit(solution)/shard_map/ppermute | solution.py:13
  39.5 0.1 collective-permute-start.2
  39.6 0.7 constant_dynamic-update-slice_fusion.6
  40.3 0.7 constant_dynamic-update-slice_fusion.5
  41.0 27.3 %collective-permute-done.2 = bf16[512,512]{1,0:T(8,128)(2,1)S(1)} collective-permute-done((bf16[512,512]{1,0:T(8,128)(2,1)S(1)}, bf16[512,512]{1,0:T(8,128)(2,1)S(1)}, u32[]{:S(2)}, u32[]{:S(2)}) %collective-permute-start.2) | collective-permute-done | bytes 524320 | tf_op jit(solution)/shard_map/ppermute | solution.py:13
  68.2 0.8 constant_dynamic-update-slice_fusion.4
  69.1 0.7 constant_dynamic-update-slice_fusion.3
  69.7 0.7 constant_dynamic-update-slice_fusion.2
  70.4 0.7 constant_dynamic-update-slice_fusion.1
  71.1 0.8 constant_dynamic-update-slice_fusion
  72.0 3.0 %fusion.7 = f32[512,512]{1,0:T(8,128)} fusion(bf16[2048,512]{1,0:T(8,128)(2,1)} %constant_dynamic-update-slice_fusion, s32[]{:T(128)S(6)} %select_n.22, s32[1024]{0:T(1024)S(1)} %broadcast_bitcast_fusion, pred[1024]{0:T(1024)(128)(4,1)S(1)} %broadcast_bitcast_fusion.1, pred[1024]{0:T(1024)(128)(4,1)S(1)} %broadcast_bitcast_fusion.2, ...), kind=kOutput, calls=%fused_computation.9 | convolution fusion | flops 538968064 | bytes 3151876 | tf_op jit(solution)/shard_map/dot_general | solution.py:41
  75.0 0.7 fusion.25
  75.6 24.6 %reduce-scatter.5.cloned.1.call-done = bf16[128,512]{1,0:T(8,128)(2,1)} async-done(((bf16[1024,512]{1,0:T(8,128)(2,1)}), bf16[128,512]{1,0:T(8,128)(2,1)}) %reduce-scatter.5.cloned.1.call-update) | async-done | bytes 131088 | tf_op jit(solution)/shard_map/reduce_scatter | solution.py:43
  100.2 26.6 %reduce-scatter.3.cloned.1.call-done = f32[128,512]{1,0:T(8,128)} async-done(((f32[512,512]{1,0:T(8,128)}), f32[128,512]{1,0:T(8,128)}) %reduce-scatter.3.cloned.1.call-update) | async-done | bytes 262160 | tf_op jit(solution)/shard_map/reduce_scatter | solution.py:51
  126.9 3.1 %multiply_add_fusion = f32[128,512]{1,0:T(8,128)} fusion(bf16[128,512]{1,0:T(8,128)(2,1)S(1)} %get-tuple-element.6, f32[128,512]{1,0:T(8,128)} %reduce-scatter.3.cloned.1.call-done, bf16[128,512]{1,0:T(8,128)(2,1)} %reduce-scatter.5.cloned.1.call-done, f32[]{:T(128)} %bitcast.4, f32[]{:T(128)} %bitcast), kind=kLoop, calls=%fused_computation.25 | loop fusion | flops 393216 | bytes 786440 | tf_op jit(solution)/shard_map/add | solution.py:52
  (12 shorter events, 0.1 us)
Async XLA Ops:
  6.5 93.7 %reduce-scatter.5.cloned.1.call-start = ((), (), s32[]{:S(2)}) async-start(), calls=%async_computation.3 | async-start | bytes 1179648 | tf_op jit(solution)/shard_map/reduce_scatter | solution.py:43
  20.1 106.8 %reduce-scatter.3.cloned.1.call-start = ((), (), s32[]{:S(2)}) async-start(), calls=%async_computation.2 | async-start | bytes 1310720 | tf_op jit(solution)/shard_map/reduce_scatter | solution.py:51
  20.1 7.9 %collective-permute-start = (bf16[128,512]{1,0:T(8,128)(2,1)S(1)}, bf16[128,512]{1,0:T(8,128)(2,1)S(1)}, u32[]{:S(2)}, u32[]{:S(2)}) collective-permute-start(bf16[128,512]{1,0:T(8,128)(2,1)S(1)} %get-tuple-element.6), channel_id=1, source_target_pairs={{0,28},{4,0},{8,4},{12,8},{16,12},{20,16},{24,20},{28,24},{1,29},{... | collective-permute-start | bytes 393224 | tf_op jit(solution)/shard_map/ppermute | solution.py:13
  28.0 11.4 %collective-permute-start.1 = (bf16[256,512]{1,0:T(8,128)(2,1)S(1)}, bf16[256,512]{1,0:T(8,128)(2,1)S(1)}, u32[]{:S(2)}, u32[]{:S(2)}) collective-permute-start(bf16[256,512]{1,0:T(8,128)(2,1)S(1)} %pad_maximum_fusion.1), channel_id=1, source_target_pairs={{0,24},{4,28},{8,0},{12,4},{16,8},{20,12},{24,16},{28,20},{1,25},{... | collective-permute-start | bytes 786440 | tf_op jit(solution)/shard_map/ppermute | solution.py:13
  39.5 32.5 %copy-start.1 = (bf16[512,8,1,128]{3,1,2,0:T(8,128)(2,1)S(1)}, bf16[512,8,1,128]{3,1,2,0:T(8,128)(2,1)}, u32[]{:S(2)}) copy-start(bf16[512,8,1,128]{3,1,2,0:T(8,128)(2,1)} %param.4) | copy-start | bytes 3145732
  39.5 28.8 %collective-permute-start.2 = (bf16[512,512]{1,0:T(8,128)(2,1)S(1)}, bf16[512,512]{1,0:T(8,128)(2,1)S(1)}, u32[]{:S(2)}, u32[]{:S(2)}) collective-permute-start(bf16[512,512]{1,0:T(8,128)(2,1)S(1)} %pad_maximum_fusion), channel_id=1, source_target_pairs={{0,16},{4,20},{8,24},{12,28},{16,0},{20,4},{24,8},{28,12},{1,17},{... | collective-permute-start | bytes 1572872 | tf_op jit(solution)/shard_map/ppermute | solution.py:13
  72.0 3.0 %copy-start = (f32[2]{0:T(128)S(1)}, f32[2]{0:T(128)}, u32[]{:S(2)}) copy-start(f32[2]{0:T(128)} %param.7) | copy-start | bytes 28
Sparse Core Ops, SparseCore 0:
  20.2 79.9 reduce-scatter.4
  102.9 23.9 reduce-scatter.2
